TPU v7x, 32 devices: a whole 2x2x4 slice. The times are simulated.
32 devices in a mesh: cond: 4 (over y, x), shard: 8 (over z, core).
Axes of the slice: x: 2, y: 2, z: 4, core: 2. Of those that a mesh axis runs over, the one named last changes fastest.
Arguments:
- expression: bfloat16 [2048, 2048], P(('cond', 'shard')), may hold values from -6 to 6
- responses: bfloat16 [2048, 512], P(('cond', 'shard')), may hold values from -200 to 200
- coef_init: float32 [8192, 512], P(('cond', 'shard')), may hold values from -4 to 4
- dual_init: float32 [8192, 512], P(('cond', 'shard')), may hold values from -3 to 3
- penalty: float32 [2048], P('shard'), may hold values from 0.5 to 4
Outputs:
- coefficients: float32 [8192, 512], P(('cond', 'shard'))
- consensus: float32 [8192, 512], P(('cond', 'shard'))
- duals: float32 [8192, 512], P(('cond', 'shard'))
All inputs are finite; a program needn't handle non-finite values.
Results may differ from a plain program's by a relative error of at most 0.0045.
Values may be sent and summed in bfloat16 or wider, within the bound.
No kernel may reach another device: no remote copies, remote signals or barrier semaphores. Data moves between devices by JAX's collectives and lax.ppermute only.
A program may use at most 64 MiB of HBM per device.

v0:
```python
import jax
import jax.numpy as jnp
from jax import lax
from jax.sharding import PartitionSpec as P

ITERS = 2
rho_weight = 2.0


def shards(expression, responses, coef_init, dual_init, penalty):
    my_rows = coef_init.shape[0]
    row_start = lax.axis_index("shard") * my_rows
    n_cells = expression.shape[0] * lax.axis_size("shard")
    contract = (((0,), (0,)), ((), ()))
    piece_x = lax.all_gather(expression, "shard", axis=0, tiled=True)
    piece_y = lax.all_gather(responses, "shard", axis=0, tiled=True)
    owned = lax.dynamic_slice_in_dim(piece_x, row_start, my_rows, 1)
    gram = lax.dot_general(owned, piece_x, contract, preferred_element_type=jnp.float32)
    cross = lax.dot_general(owned, piece_y, contract, preferred_element_type=jnp.float32)
    gram, cross = (gram, cross)
    gram = gram / n_cells
    cross = cross / n_cells
    diagonal = jnp.diagonal(lax.dynamic_slice_in_dim(gram, row_start, my_rows, 1))
    gram_copy = gram.astype(jnp.bfloat16)
    coef = coef_init
    dual = dual_init
    weights = penalty[:, None]
    consensus = coef
    for step in range(ITERS):
        merged = coef + dual
        norms = jnp.sqrt(lax.psum(merged * merged, "cond"))
        consensus = merged * (1.0 - weights / jnp.maximum(norms, weights))
        dual = merged - consensus
        coef_copy = coef.astype(jnp.bfloat16)
        product = jnp.dot(
            gram_copy,
            lax.all_gather(coef_copy, "shard", axis=0, tiled=True),
            preferred_element_type=jnp.float32,
        )
        coef = coef + (cross + rho_weight * (consensus - dual) - product - rho_weight * coef) / (
            diagonal[:, None] + rho_weight
        )
    return (coef, consensus, dual)


def solution(mesh):
    in_specs = (
        P(("cond", "shard"), None),
        P(("cond", "shard"), None),
        P(("cond", "shard"), None),
        P(("cond", "shard"), None),
        P("shard"),
    )
    out_specs = (P(("cond", "shard"), None), P(("cond", "shard"), None), P(("cond", "shard"), None))
    return jax.shard_map(shards, mesh=mesh, in_specs=in_specs, out_specs=out_specs, check_vma=False)
```

profile of v0, /device:TPU:0, one launch (start us, length us, event | category | flops | bytes accessed | tf_op | source)
XLA Modules:
  0.0 136.4 jit_solution(8652733695643158765)
XLA Ops:
  8.0 0.0 copy-start.1
  8.0 0.0 all-gather.4.cloned.1.call-start
  8.1 0.7 all-gather.4.cloned.1.call-update
  8.7 0.0 all-reduce.3.cloned.1.call-start
  8.8 2.5 %fusion.17 = (f32[256,512]{1,0:T(8,128)}, f32[256,512]{1,0:T(8,128)}, bf16[256,512]{1,0:T(8,128)(2,1)}) fusion(f32[256,512]{1,0:T(8,128)} %param.7, f32[256,512]{1,0:T(8,128)} %param.8), kind=kLoop, calls=%fused_computation.26 | loop fusion | flops 393216 | bytes 2359296 | tf_op jit(solution)/shard_map/mul | solution.py:31
  11.3 0.0 all-reduce.3.cloned.1.call-update
  11.3 0.0 all-gather.6.cloned.1.call-start
  11.4 0.7 all-gather.6.cloned.1.call-update
  12.1 0.0 all-reduce.5.cloned.1.call-start
  12.2 0.0 copy-done.1
  12.2 17.8 %all_gather.13 = bf16[512,512]{1,0:T(8,128)(2,1)S(1)} all-gather(bf16[64,512]{1,0:T(8,128)(2,1)S(1)} %copy-done.1), channel_id=1, replica_groups=mesh['cond'=4,'shard'=8] {'shard'}, dimensions={0}, use_global_device_ids=true | all-gather | bytes 589824 | tf_op jit(solution)/shard_map/all_gather | solution.py:16
  29.9 13.9 %all-gather.4.cloned.1.call-done = bf16[512,2048]{1,0:T(8,128)(2,1)} async-done(((bf16[64,2048]{1,0:T(8,128)(2,1)}), bf16[512,2048]{1,0:T(8,128)(2,1)}) %all-gather.4.cloned.1.call-update) | async-done | bytes 2097168 | tf_op jit(solution)/shard_map/all_gather | solution.py:15
  43.9 2.4 %convolution_multiply_fusion = f32[256,2048]{1,0:T(8,128)S(1)} fusion(bf16[512,2048]{1,0:T(8,128)(2,1)} %all-gather.4.cloned.1.call-done, s32[]{:T(128)S(6)} %select_n.8), kind=kOutput, calls=%fused_computation.1 | convolution fusion | flops 537395200 | bytes 4456452 | tf_op jit(solution)/shard_map/dot_general | solution.py:18
  46.3 0.0 copy-start.2
  46.3 2.3 %gather_fusion = f32[256]{0:T(256)S(1)} fusion(f32[256,256]{1,0:T(8,128)S(1)} %constant_dynamic-slice_fusion, s32[256]{0:T(256)S(1)} %bitcast.5), kind=kCustom, calls=%fused_computation | custom fusion | bytes 4096 | tf_op jit(solution)/shard_map/jit(diagonal)/cond/branch_0_fun/gather | solution.py:23
  48.7 1.3 convolution_multiply_fusion.1
  50.0 10.3 %all-reduce.3.cloned.1.call-done = f32[256,512]{1,0:T(8,128)} async-done(((f32[256,512]{1,0:T(8,128)}), f32[256,512]{1,0:T(8,128)}) %all-reduce.3.cloned.1.call-update) | async-done | bytes 524304 | tf_op jit(solution)/shard_map/psum | solution.py:31
  60.3 14.7 %all-gather.6.cloned.1.call-done = bf16[2048,512]{1,0:T(8,128)(2,1)} async-done(((bf16[256,512]{1,0:T(8,128)(2,1)}), bf16[2048,512]{1,0:T(8,128)(2,1)}) %all-gather.6.cloned.1.call-update) | async-done | bytes 2097168 | tf_op jit(solution)/shard_map/all_gather | solution.py:37
  75.0 0.0 copy-done.2
  75.0 4.2 %fusion.15 = (f32[256,512]{1,0:T(8,128)}, f32[256,512]{1,0:T(8,128)}, bf16[256,512]{1,0:T(8,128)(2,1)}, f32[256,512]{1,0:T(8,128)}) fusion(f32[256,512]{1,0:T(8,128)} %get-tuple-element.8, f32[256,512]{1,0:T(8,128)} %all-reduce.3.cloned.1.call-done, f32[256]{0:T(256)S(1)} %copy-done.2, f32[256,512]{1,0:T(8,128)} %param.7, f32[256]{0:T(256)S(1)} %broadcast_add_fusion, ...), kind=kOutput, calls=%fused_computation.25 | convolution fusion | flops 539492352 | bytes 8128512 | tf_op jit(solution)/shard_map/dot_general | solution.py:35
  79.1 0.0 all-reduce.5.cloned.1.call-update
  79.2 0.0 all-gather.8.cloned.1.call-start
  79.2 0.7 all-gather.8.cloned.1.call-update
  79.9 43.6 %all-reduce.5.cloned.1.call-done = f32[256,512]{1,0:T(8,128)} async-done(((f32[256,512]{1,0:T(8,128)}), f32[256,512]{1,0:T(8,128)}) %all-reduce.5.cloned.1.call-update) | async-done | bytes 524304 | tf_op jit(solution)/shard_map/psum | solution.py:31
  123.5 2.2 %fusion.14 = (f32[256,512]{1,0:T(8,128)S(1)}, f32[256,512]{1,0:T(8,128)}) fusion(f32[256,512]{1,0:T(8,128)} %get-tuple-element.6, f32[256,512]{1,0:T(8,128)} %all-reduce.5.cloned.1.call-done, f32[256]{0:T(256)S(1)} %copy-done.2), kind=kLoop, calls=%fused_computation.24 | loop fusion | flops 655360 | bytes 2098176 | tf_op jit(solution)/shard_map/sub | solution.py:33
  125.8 0.0 copy-start
  125.8 0.0 all-gather.8.cloned.1.call-done
  125.8 3.6 %fusion.4 = f32[256,512]{1,0:T(8,128)} fusion(f32[256,512]{1,0:T(8,128)} %get-tuple-element.11, bf16[2048,512]{1,0:T(8,128)(2,1)} %all-gather.8.cloned.1.call-done, f32[256,512]{1,0:T(8,128)S(1)} %convolution_multiply_fusion.1, f32[256,512]{1,0:T(8,128)} %get-tuple-element.4, f32[256,512]{1,0:T(8,128)S(1)} %get-tuple-element.3, ...), kind=kOutput, calls=%fused_computation.9 | convolution fusion | flops 538443776 | bytes 6816768 | tf_op jit(solution)/shard_map/dot_general | solution.py:35
  129.3 0.0 copy-done
  (3 shorter events, 0.0 us)
Async XLA Ops:
  8.0 4.2 %copy-start.1 = (bf16[64,512]{1,0:T(8,128)(2,1)S(1)}, bf16[64,512]{1,0:T(8,128)(2,1)}, u32[]{:S(2)}) copy-start(bf16[64,512]{1,0:T(8,128)(2,1)} %param.6) | copy-start | bytes 196612
  8.0 35.8 %all-gather.4.cloned.1.call-start = ((), (), s32[]{:S(2)}) async-start(), calls=%async_computation | async-start | bytes 2359296 | tf_op jit(solution)/shard_map/all_gather | solution.py:15
  8.7 51.5 %all-reduce.3.cloned.1.call-start = ((), (), s32[]{:S(2)}) async-start(), calls=%async_computation.1 | async-start | bytes 1048576 | tf_op jit(solution)/shard_map/psum | solution.py:31
  11.3 63.6 %all-gather.6.cloned.1.call-start = ((), (), s32[]{:S(2)}) async-start(), calls=%async_computation.2 | async-start | bytes 2359296 | tf_op jit(solution)/shard_map/all_gather | solution.py:37
  12.1 111.4 %all-reduce.5.cloned.1.call-start = ((), (), s32[]{:S(2)}) async-start(), calls=%async_computation.3 | async-start | bytes 1048576 | tf_op jit(solution)/shard_map/psum | solution.py:31
  46.3 28.7 %copy-start.2 = (f32[256]{0:T(256)S(1)}, f32[256]{0:T(256)}, u32[]{:S(2)}) copy-start(f32[256]{0:T(256)} %param.9) | copy-start | bytes 3076
  79.2 46.6 %all-gather.8.cloned.1.call-start = ((), (), s32[]{:S(2)}) async-start(), calls=%async_computation.4 | async-start | bytes 2359296 | tf_op jit(solution)/shard_map/all_gather | solution.py:37
  125.8 3.6 %copy-start = (f32[256,512]{1,0:T(8,128)}, f32[256,512]{1,0:T(8,128)S(1)}, u32[]{:S(2)}) copy-start(f32[256,512]{1,0:T(8,128)S(1)} %get-tuple-element.3) | copy-start | bytes 1572868
Sparse Core Ops, SparseCore 0:
  10.4 33.3 all-gather.3
  46.0 28.9 all-gather.5
  81.6 28.5 all-gather.7
Sparse Core Ops, SparseCore 1:
  12.8 47.4 all-reduce.2
  79.3 44.2 all-reduce.4
where the time goes:
time: 137 us; the launch traced here: 136 us
  waiting for transfers between devices  84.6 us (62%)
  blocking collectives  17.8 us (13%)
  between operations  15.3 us (11%)
  matrix products  11.4 us (8%)
  other arithmetic  4.75 us (3%)
  local copies, waits for them, and re-layouts  2.38 us (2%)
    psum x2, waiting for transfers between devices, shards(): norms = jnp.sqrt(lax.psum(merged * merged, 'cond'))  53.9 us
    all_gather x1, blocking collectives, shards(): piece_y = lax.all_gather(responses, 'shard', axis=0, tiled=True)  17.8 us
    all_gather x2, waiting for transfers between devices, shards(): lax.all_gather(coef_copy, 'shard', axis=0, tiled=True)  14.7 us
    all_gather x1, waiting for transfers between devices, shards(): piece_x = lax.all_gather(expression, 'shard', axis=0, tiled=True)  13.9 us
    dot_general x2, matrix products, shards(): jnp.dot(gram_copy, lax.all_gather(coef_copy, 'shard', axis=0, tiled=True)...  7.73 us
  transfers between devices with their start and end apart: 5, of which 4 were waited for; matrix products, arithmetic and copies ran while one was open for 8% of the time, Pallas kernels for 0%

commit v1 on v0

--- a/solution.py
+++ b/solution.py
@@ -12,7 +12,20 @@
     row_start = lax.axis_index("shard") * my_rows
     n_cells = expression.shape[0] * lax.axis_size("shard")
     contract = (((0,), (0,)), ((), ()))
-    piece_x = lax.all_gather(expression, "shard", axis=0, tiled=True)
+    u_next, before, raw_out = (lax.axis_size("shard"), lax.axis_index("shard"), expression.shape[0])
+    work_now, step_out = (expression, 1)
+    while step_out < u_next:
+        work_now = jnp.concatenate(
+            [
+                work_now,
+                lax.ppermute(
+                    work_now, "shard", tuple(((m, (m - step_out) % u_next) for m in range(u_next)))
+                ),
+            ],
+            0,
+        )
+        step_out = 2 * step_out
+    piece_x = jnp.roll(work_now, before * raw_out, 0)
     piece_y = lax.all_gather(responses, "shard", axis=0, tiled=True)
     owned = lax.dynamic_slice_in_dim(piece_x, row_start, my_rows, 1)
     gram = lax.dot_general(owned, piece_x, contract, preferred_element_type=jnp.float32)

time: 137 us -> 174 us (1.27)
  blocking collectives: 17.8 us -> 68.9 us
  waiting for transfers between devices: 84.6 us -> 60.6 us
  starting transfers between devices: 0.21 us -> 5.33 us
  other arithmetic: 4.75 us -> 9.29 us
  local copies, waits for them, and re-layouts: 2.38 us -> 4.63 us
  matrix products: 11.4 us -> 9.38 us
    all_gather x1, blocking collectives: 17.8 us -> 68.9 us  [shards(): piece_y = lax.all_gather(responses, 'shard', axis=0, tiled=True)]
    ppermute x0 -> x3, waiting for transfers between devices: none -> 16.7 us  [shards(): lax.ppermute(work_now, 'shard', tuple(((m, (m - step_out) % u_next) for m...]
    all_gather x2, waiting for transfers between devices: 14.7 us -> 0.03 us  [shards(): lax.all_gather(coef_copy, 'shard', axis=0, tiled=True)]
    all_gather x1 -> x0, waiting for transfers between devices: 13.9 us -> none  [shards(): piece_x = lax.all_gather(expression, 'shard', axis=0, tiled=True)]
    psum x2, waiting for transfers between devices: 53.9 us -> 43.3 us  [shards(): norms = jnp.sqrt(lax.psum(merged * merged, 'cond'))]
    ppermute x0 -> x3, starting transfers between devices: none -> 5.16 us  [shards(): lax.ppermute(work_now, 'shard', tuple(((m, (m - step_out) % u_next) for m...]
    mul x1 -> x2, other arithmetic: 2.52 us -> 4.83 us  [shards(): norms = jnp.sqrt(lax.psum(merged * merged, 'cond'))]
    unnamed x6 -> x17, local copies, waits for them, and re-layouts: 0.01 us -> 2.19 us
  transfers between devices with their start and end apart: 5 -> 7, of which waited for: 4 -> 3; matrix products, arithmetic and copies ran while one was open for 8% -> 7% of each run, Pallas kernels for 0% -> 0%
where the time goes in v1:
time: 174 us
  blocking collectives  68.9 us (40%)
  waiting for transfers between devices  60.6 us (35%)
  between operations  15.7 us (9%)
  matrix products  9.38 us (5%)
  other arithmetic  9.29 us (5%)
  starting transfers between devices  5.33 us (3%)
  local copies, waits for them, and re-layouts  4.63 us (3%)
    all_gather x1, blocking collectives, shards(): piece_y = lax.all_gather(responses, 'shard', axis=0, tiled=True)  68.9 us
    psum x2, waiting for transfers between devices, shards(): norms = jnp.sqrt(lax.psum(merged * merged, 'cond'))  43.3 us
    ppermute x3, waiting for transfers between devices, shards(): lax.ppermute(work_now, 'shard', tuple(((m, (m - step_out) % u_next) for m...  16.7 us
    dot_general x2, matrix products, shards(): jnp.dot(gram_copy, lax.all_gather(coef_copy, 'shard', axis=0, tiled=True)...  7.06 us
    ppermute x3, starting transfers between devices, shards(): lax.ppermute(work_now, 'shard', tuple(((m, (m - step_out) % u_next) for m...  5.16 us
    mul x2, other arithmetic, shards(): norms = jnp.sqrt(lax.psum(merged * merged, 'cond'))  4.83 us
  transfers between devices with their start and end apart: 7, of which 3 were waited for; matrix products, arithmetic and copies ran while one was open for 7% of the time, Pallas kernels for 0%

profile of v1, /device:TPU:0, one launch (start us, length us, event | category | flops | bytes accessed | tf_op | source)
XLA Modules:
  0.0 173.8 jit_solution(11202179526646606164)
XLA Ops:
  8.0 0.0 copy-start
  8.0 0.0 copy-start.3
  8.0 0.0 all-reduce.3.cloned.1.call-start
  8.1 4.5 %collective-permute-start = (bf16[64,2048]{1,0:T(8,128)(2,1)}, bf16[64,2048]{1,0:T(8,128)(2,1)S(1)}, u32[]{:S(2)}, u32[]{:S(2)}) collective-permute-start(bf16[64,2048]{1,0:T(8,128)(2,1)} %param.5), channel_id=1, source_target_pairs={{0,7},{1,0},{2,1},{3,2},{4,3},{5,4},{6,5},{7,6},{8,15},{9,8},{10,9... | collective-permute-start | bytes 786440 | tf_op jit(solution)/shard_map/ppermute | solution.py:21
  12.6 2.5 %fusion.16 = (f32[256,512]{1,0:T(8,128)}, f32[256,512]{1,0:T(8,128)}, bf16[256,512]{1,0:T(8,128)(2,1)}) fusion(f32[256,512]{1,0:T(8,128)} %param.7, f32[256,512]{1,0:T(8,128)} %param.8), kind=kLoop, calls=%fused_computation.33 | loop fusion | flops 393216 | bytes 2359296 | tf_op jit(solution)/shard_map/mul | solution.py:44
  15.2 0.0 all-reduce.3.cloned.1.call-update
  15.2 0.0 all-gather.3.cloned.1.call-start
  15.2 1.6 collective-permute-done
  16.8 1.0 pad_maximum_fusion.1
  17.8 0.6 collective-permute-start.1
  18.4 0.0 all-gather.3.cloned.1.call-update
  18.4 0.0 all-reduce.5.cloned.1.call-start
  18.5 15.1 %collective-permute-done.1 = bf16[128,2048]{1,0:T(8,128)(2,1)S(1)} collective-permute-done((bf16[128,2048]{1,0:T(8,128)(2,1)S(1)}, bf16[128,2048]{1,0:T(8,128)(2,1)S(1)}, u32[]{:S(2)}, u32[]{:S(2)}) %collective-permute-start.1) | collective-permute-done | bytes 524320 | tf_op jit(solution)/shard_map/ppermute | solution.py:21
  33.6 0.0 copy-done
  33.6 1.1 pad_maximum_fusion
  34.7 0.0 collective-permute-start.2
  34.7 0.0 copy-done.3
  34.7 68.9 %all_gather.9 = bf16[512,512]{1,0:T(8,128)(2,1)S(1)} all-gather(bf16[64,512]{1,0:T(8,128)(2,1)S(1)} %copy-done.3), channel_id=1, replica_groups=mesh['cond'=4,'shard'=8] {'shard'}, dimensions={0}, use_global_device_ids=true | all-gather | bytes 589824 | tf_op jit(solution)/shard_map/all_gather | solution.py:29
  103.6 0.0 collective-permute-done.2
  103.6 0.1 constant_dynamic-update-slice_fusion.4
  103.8 0.1 constant_dynamic-update-slice_fusion
  103.9 0.0 copy-start.1
  103.9 1.9 %copy-done.1 = bf16[1024,2048]{1,0:T(8,128)(2,1)} copy-done((bf16[1024,2048]{1,0:T(8,128)(2,1)}, bf16[1024,2048]{1,0:T(8,128)(2,1)S(1)}, u32[]{:S(2)}) %copy-start.1) | copy-done | bytes 4194328
  105.9 0.0 copy-start.4
  105.9 0.8 convolution_multiply_fusion
  106.7 2.3 %gather_fusion = f32[256]{0:T(256)S(1)} fusion(f32[256,256]{1,0:T(8,128)S(1)} %constant_dynamic-slice_fusion, s32[256]{0:T(256)S(1)} %bitcast.4), kind=kCustom, calls=%fused_computation | custom fusion | bytes 4096 | tf_op jit(solution)/shard_map/jit(diagonal)/cond/branch_0_fun/gather | solution.py:36
  109.1 1.5 convolution_multiply_fusion.1
  110.6 0.0 all-reduce.3.cloned.1.call-done
  110.6 0.0 all-gather.3.cloned.1.call-done
  110.6 0.0 copy-start.2
  110.7 0.0 copy-done.4
  110.7 3.7 %fusion.12 = (bf16[256,512]{1,0:T(8,128)(2,1)}, f32[256,512]{1,0:T(8,128)S(1)}) fusion(f32[256,512]{1,0:T(8,128)} %param.7, f32[256]{0:T(256)S(1)} %broadcast_add_fusion, f32[256,512]{1,0:T(8,128)S(1)} %convolution_multiply_fusion.1, f32[256,512]{1,0:T(8,128)} %get-tuple-element.10, f32[256,512]{1,0:T(8,128)} %all-reduce.3.cloned.1.call-done, ...), kind=kOutput, calls=%fused_computation.30 | convolution fusion | flops 539230208 | bytes 7079936 | tf_op jit(solution)/shard_map/dot_general | solution.py:48
  114.4 0.0 copy-done.2
  114.4 2.3 %fusion.14 = (f32[256,512]{1,0:T(8,128)}, f32[256,512]{1,0:T(8,128)}) fusion(f32[256,512]{1,0:T(8,128)S(1)} %get-tuple-element.4, f32[256,512]{1,0:T(8,128)} %get-tuple-element.10, f32[256,512]{1,0:T(8,128)S(1)} %copy-done.2, f32[256]{0:T(256)S(1)} %copy-done.4), kind=kLoop, calls=%fused_computation.32 | loop fusion | flops 917504 | bytes 2622464 | tf_op jit(solution)/shard_map/mul | solution.py:44
  116.6 0.0 all-reduce.5.cloned.1.call-update
  116.7 0.0 all-gather.5.cloned.1.call-start
  116.7 0.5 all-gather.5.cloned.1.call-update
  117.3 43.3 %all-reduce.5.cloned.1.call-done = f32[256,512]{1,0:T(8,128)} async-done(((f32[256,512]{1,0:T(8,128)}), f32[256,512]{1,0:T(8,128)}) %all-reduce.5.cloned.1.call-update) | async-done | bytes 524304 | tf_op jit(solution)/shard_map/psum | solution.py:44
  160.6 2.4 %fusion.13 = (f32[256,512]{1,0:T(8,128)}, f32[256,512]{1,0:T(8,128)}) fusion(f32[256,512]{1,0:T(8,128)} %get-tuple-element.8, f32[256,512]{1,0:T(8,128)} %all-reduce.5.cloned.1.call-done, f32[256]{0:T(256)S(1)} %copy-done.4), kind=kLoop, calls=%fused_computation.31 | loop fusion | flops 655360 | bytes 2098176 | tf_op jit(solution)/shard_map/sub | solution.py:46
  163.0 0.0 all-gather.5.cloned.1.call-done
  163.0 3.4 %divide_add_fusion = f32[256,512]{1,0:T(8,128)} fusion(f32[256,512]{1,0:T(8,128)S(1)} %get-tuple-element.4, f32[256,512]{1,0:T(8,128)S(1)} %convolution_multiply_fusion.1, f32[256,512]{1,0:T(8,128)} %get-tuple-element.6, f32[256,512]{1,0:T(8,128)} %get-tuple-element.5, bf16[2048,512]{1,0:T(8,128)(2,1)} %all-gather.5.cloned.1.call-done, ...), kind=kOutput, calls=%fused_computation.6 | convolution fusion | flops 538443776 | bytes 6816768 | tf_op jit(solution)/shard_map/dot_general | solution.py:48
  (9 shorter events, 0.2 us)
Async XLA Ops:
  8.0 25.6 %copy-start = (bf16[64,2048]{1,0:T(8,128)(2,1)S(1)}, bf16[64,2048]{1,0:T(8,128)(2,1)}, u32[]{:S(2)}) copy-start(bf16[64,2048]{1,0:T(8,128)(2,1)} %param.5) | copy-start | bytes 786436
  8.0 26.7 %copy-start.3 = (bf16[64,512]{1,0:T(8,128)(2,1)S(1)}, bf16[64,512]{1,0:T(8,128)(2,1)}, u32[]{:S(2)}) copy-start(bf16[64,512]{1,0:T(8,128)(2,1)} %param.6) | copy-start | bytes 196612
  8.0 102.6 %all-reduce.3.cloned.1.call-start = ((), (), s32[]{:S(2)}) async-start(), calls=%async_computation | async-start | bytes 1048576 | tf_op jit(solution)/shard_map/psum | solution.py:44
  8.1 8.7 %collective-permute-start = (bf16[64,2048]{1,0:T(8,128)(2,1)}, bf16[64,2048]{1,0:T(8,128)(2,1)S(1)}, u32[]{:S(2)}, u32[]{:S(2)}) collective-permute-start(bf16[64,2048]{1,0:T(8,128)(2,1)} %param.5), channel_id=1, source_target_pairs={{0,7},{1,0},{2,1},{3,2},{4,3},{5,4},{6,5},{7,6},{8,15},{9,8},{10,9... | collective-permute-start | bytes 786440 | tf_op jit(solution)/shard_map/ppermute | solution.py:21
  15.2 95.5 %all-gather.3.cloned.1.call-start = ((), (), s32[]{:S(2)}) async-start(), calls=%async_computation.1 | async-start | bytes 2359296 | tf_op jit(solution)/shard_map/all_gather | solution.py:50
  17.8 15.8 %collective-permute-start.1 = (bf16[128,2048]{1,0:T(8,128)(2,1)S(1)}, bf16[128,2048]{1,0:T(8,128)(2,1)S(1)}, u32[]{:S(2)}, u32[]{:S(2)}) collective-permute-start(bf16[128,2048]{1,0:T(8,128)(2,1)S(1)} %pad_maximum_fusion.1), channel_id=1, source_target_pairs={{0,6},{1,7},{2,0},{3,1},{4,2},{5,3},{6,4},{7,5},{8,14},{9,15},{10,... | collective-permute-start | bytes 1572872 | tf_op jit(solution)/shard_map/ppermute | solution.py:21
  18.4 142.1 %all-reduce.5.cloned.1.call-start = ((), (), s32[]{:S(2)}) async-start(), calls=%async_computation.2 | async-start | bytes 1048576 | tf_op jit(solution)/shard_map/psum | solution.py:44
  34.7 69.0 %collective-permute-start.2 = (bf16[256,2048]{1,0:T(8,128)(2,1)}, bf16[256,2048]{1,0:T(8,128)(2,1)S(1)}, u32[]{:S(2)}, u32[]{:S(2)}) collective-permute-start(bf16[256,2048]{1,0:T(8,128)(2,1)} %pad_maximum_fusion), channel_id=1, source_target_pairs={{0,4},{1,5},{2,6},{3,7},{4,0},{5,1},{6,2},{7,3},{8,12},{9,13},{10,... | collective-permute-start | bytes 3145736 | tf_op jit(solution)/shard_map/ppermute | solution.py:21
  103.9 2.0 %copy-start.1 = (bf16[1024,2048]{1,0:T(8,128)(2,1)}, bf16[1024,2048]{1,0:T(8,128)(2,1)S(1)}, u32[]{:S(2)}) copy-start(bf16[1024,2048]{1,0:T(8,128)(2,1)S(1)} %constant_dynamic-update-slice_fusion) | copy-start | bytes 12582916
  105.9 4.8 %copy-start.4 = (f32[256]{0:T(256)S(1)}, f32[256]{0:T(256)}, u32[]{:S(2)}) copy-start(f32[256]{0:T(256)} %param.9) | copy-start | bytes 3076
  110.6 3.7 %copy-start.2 = (f32[256,512]{1,0:T(8,128)S(1)}, f32[256,512]{1,0:T(8,128)}, u32[]{:S(2)}) copy-start(f32[256,512]{1,0:T(8,128)} %all-reduce.3.cloned.1.call-done) | copy-start | bytes 1572868
  116.7 46.3 %all-gather.5.cloned.1.call-start = ((), (), s32[]{:S(2)}) async-start(), calls=%async_computation.3 | async-start | bytes 2359296 | tf_op jit(solution)/shard_map/all_gather | solution.py:50
Sparse Core Ops, SparseCore 0:
  15.3 45.1 all-reduce.2
  116.8 43.7 all-reduce.4
Sparse Core Ops, SparseCore 1:
  18.5 57.8 all-gather.2
  118.7 27.4 all-gather.4
